TPU v7x, 512 devices: a whole 4x4x16 slice. The times are simulated.
512 devices in a mesh: seq: 128 (over y, x, z_lo, core), batch: 4 (over z_hi).
Axes of the slice: x: 4, y: 4, z: 16 (z_hi: 4, z_lo: 4; z = z_hi * 4 + z_lo), core: 2. Of those that a mesh axis runs over, the one named last changes fastest.
Arguments:
- values: bfloat16 [1, 32768, 512], P(None, 'seq', 'batch'), may hold values from -6 to 6
- gate_in: bfloat16 [1, 32768, 512], P(None, 'seq', 'batch'), may hold values from -6 to 6
- gate_out: bfloat16 [1, 32768, 512], P(None, 'seq', 'batch'), may hold values from -6 to 6
- cotangent: bfloat16 [1, 32768, 512], P(None, 'seq', 'batch'), may hold values from -6 to 6
- filters: float32 [64, 32768], P(None, 'seq'), may hold values from -0.03125 to 0.03125
Outputs:
- grad_values: bfloat16 [1, 32768, 512], P(None, 'seq', 'batch')
- grad_gate_in: bfloat16 [1, 32768, 512], P(None, 'seq', 'batch')
- grad_gate_out: bfloat16 [1, 32768, 512], P(None, 'seq', 'batch')
- grad_filters: float32 [64, 32768], P('batch', 'seq')
All inputs are finite; a program needn't handle non-finite values.
Results may differ from a plain program's by a relative error of at most 0.012.
Values may be sent and summed in bfloat16 or wider, within the bound.
No kernel may reach another device: no remote copies, remote signals or barrier semaphores. Data moves between devices by JAX's collectives and lax.ppermute only.
A program may use at most 64 MiB of HBM per device.

v0:
```python
import math

import jax
import jax.numpy as jnp
import ml_dtypes
import numpy as np
from jax import lax
from jax.experimental import pallas as pl
from jax.experimental.pallas import tpu as pltpu
from jax.sharding import PartitionSpec as P

F32 = jnp.float32
BF16 = jnp.bfloat16


def tables(rows, cols):
    n = rows * cols
    theta = 2.0 * np.pi * np.outer(np.arange(rows) + 0.25, np.arange(rows)) / rows
    first = np.concatenate([np.cos(theta), -np.sin(theta)], 0)
    phi = 2.0 * np.pi * np.outer(np.arange(rows) + 0.25, np.arange(cols)) / n
    turn = np.concatenate([np.cos(phi), np.sin(phi)], 1)
    angle = 2.0 * np.pi * (np.outer(np.arange(cols), np.arange(cols)) % cols) / cols
    c, s = np.cos(angle), np.sin(angle)
    inner = np.block([[c, -s], [s, c]])

    def short(a):
        return a.astype(np.float32).astype(ml_dtypes.bfloat16)

    return (
        short(first),
        short(np.ascontiguousarray(first.T)),
        turn.astype(np.float32),
        short(inner),
        short(np.ascontiguousarray(inner.T)),
    )


def dot(a, b):
    return jnp.dot(a, b, preferred_element_type=F32)


def vmem_call(kernel, out_shape, flops, size):
    return pl.pallas_call(
        kernel,
        out_shape=out_shape,
        cost_estimate=pl.CostEstimate(flops=flops, bytes_accessed=size, transcendentals=0),
    )


def gather_kernel(values, gate_in, gate_out, cotangent, filters, out):
    half = out.shape[1] // 6
    taps = filters.shape[0]
    for part, (a, b) in enumerate(((values, gate_in), (cotangent, gate_out))):
        product = a[...].astype(F32) * b[...].astype(F32)
        for side in range(2):
            piece = product[side * half : (side + 1) * half].T
            at = (3 * side + part) * half
            out[:, at : at + half] = piece.astype(BF16)
    for side in range(2):
        piece = filters[:, side * half : (side + 1) * half].astype(BF16)
        at = (3 * side + 2) * half
        for copy in range(out.shape[0] // taps):
            out[copy * taps : (copy + 1) * taps, at : at + half] = piece


def spectra_kernel(scale, sent, first, first_t, turn, inner, inner_t, out):
    rows = out.shape[0]
    cols = out.shape[1] // 3
    half = cols // 2
    wc, ws = turn[:, :cols], turn[:, cols:]
    a = dot(first[...], sent[...])
    specs = []
    for j in range(3):
        at = [slice(j * half, (j + 1) * half), slice((3 + j) * half, (4 + j) * half)]
        re = jnp.concatenate([a[:rows, at[0]], a[:rows, at[1]]], axis=1)
        im = jnp.concatenate([a[rows:, at[0]], a[rows:, at[1]]], axis=1)
        b = jnp.concatenate([re * wc + im * ws, im * wc - re * ws], axis=1)
        f = dot(b.astype(BF16), inner[...])
        specs.append((f[:, :cols], f[:, cols:]))
    (xr, xi), (gr, gi), (hr, hi) = specs
    products = (
        (hr * xr - hi * xi, hr * xi + hi * xr, 1.0),
        (hr * gr + hi * gi, hr * gi - hi * gr, 1.0),
        (xr * gr + xi * gi, xr * gi - xi * gr, scale),
    )
    size = 1.0 / (rows * cols)
    for j, (pr, pi, factor) in enumerate(products):
        p = jnp.concatenate([pr, pi], axis=1).astype(BF16)
        u = dot(p, inner_t[...])
        ur, ui = u[:, :cols], u[:, cols:]
        v = jnp.concatenate([ur * wc - ui * ws, ur * ws + ui * wc], axis=0)
        y = dot(first_t[...], v.astype(BF16)) * (size * factor)
        for side in range(2):
            at = (3 * side + j) * half
            out[:, at : at + half] = y[:, side * half : (side + 1) * half].astype(BF16)


def finish_kernel(values, gate_in, cotangent, back, grad_values, grad_gate_in, grad_gate_out):
    half = back.shape[1] // 6
    for side in range(2):
        at = slice(side * half, (side + 1) * half)
        lo = 3 * side * half
        conv = back[:, lo : lo + half].astype(F32).T
        corr = back[:, lo + half : lo + 2 * half].astype(F32).T
        grad_values[at] = (gate_in[at].astype(F32) * corr).astype(BF16)
        grad_gate_in[at] = (values[at].astype(F32) * corr).astype(BF16)
        grad_gate_out[at] = (cotangent[at].astype(F32) * conv).astype(BF16)


def body(values, gate_in, gate_out, cotangent, filters):
    values, gate_in, gate_out, cotangent = (x[0] for x in (values, gate_in, gate_out, cotangent))
    cols, channels = values.shape
    shards = lax.axis_size("seq")
    replicas = lax.axis_size("batch")
    taps = filters.shape[0]
    wide = 3 * cols
    first, first_t, turn, inner, inner_t = tables(shards, cols)
    scale = 1.0 / math.sqrt(channels * replicas // taps * shards * cols)

    def to_all(x):
        x = x.reshape(x.shape[0], 2, wide // 2)
        x = lax.all_to_all(x, "seq", split_axis=0, concat_axis=0, tiled=True)
        return x.reshape(x.shape[0], wide)

    pack = vmem_call(
        gather_kernel,
        jax.ShapeDtypeStruct((channels, wide), BF16),
        10 * channels * wide,
        12 * channels * wide,
    )
    sent = to_all(pack(values, gate_in, gate_out, cotangent, filters))

    def spectra(*refs):
        spectra_kernel(scale, *refs)

    transform = vmem_call(
        spectra,
        jax.ShapeDtypeStruct((shards, wide), BF16),
        4 * shards * wide * (2 * cols + shards),
        4 * shards * wide,
    )
    back = to_all(transform(sent, first, first_t, turn, inner, inner_t))

    half = cols // 2
    terms = jnp.concatenate([back[:, wide // 2 - half : wide // 2], back[:, wide - half :]], axis=1)
    per_filter = terms.astype(F32).reshape(channels // taps, taps, cols).sum(axis=0)
    parts = per_filter.astype(BF16).reshape(replicas, taps // replicas, cols)
    parts = lax.all_to_all(parts, "batch", split_axis=0, concat_axis=0, tiled=True)
    finish = vmem_call(
        finish_kernel,
        [jax.ShapeDtypeStruct((cols, channels), BF16)] * 3,
        12 * cols * channels,
        20 * cols * channels,
    )
    grads = finish(values, gate_in, cotangent, back)
    grad_filters = parts.astype(F32).sum(axis=0)
    return tuple(x[None] for x in grads) + (grad_filters,)


def solution(mesh):
    placed = P(None, "seq", "batch")
    return jax.shard_map(
        body,
        mesh=mesh,
        in_specs=(placed, placed, placed, placed, P(None, "seq")),
        out_specs=(placed, placed, placed, P("batch", "seq")),
        check_vma=False,
    )
```

profile of v0, /device:TPU:1, one launch (start us, length us, event | category | flops | bytes accessed | tf_op | source)
XLA Modules:
  0.0 76.8 jit_solution(10178284302578669578)
XLA Ops:
  0.6 1.7 %shard_map.129 = bf16[128,768]{1,0:T(8,128)(2,1)} custom-call(bf16[256,128]{1,0:T(8,128)(2,1)} %bitcast.19, bf16[256,128]{1,0:T(8,128)(2,1)} %bitcast.21, bf16[256,128]{1,0:T(8,128)(2,1)} %bitcast.27, bf16[256,128]{1,0:T(8,128)(2,1)} %bitcast.23, f32[64,256]{1,0:T(8,128)} %filters.1), custom_call_target="tpu_custom_call" | custom-call | flops 983040 | bytes 1179648 | tf_op jit(solution)/shard_map/pallas_call | solution.py:131
  2.4 1.0 %reshape.26 = bf16[128,2,384]{2,1,0:T(2,128)(2,1)S(1)} reshape(bf16[128,768]{1,0:T(8,128)(2,1)} %shard_map.129) | data formatting | bytes 393216 | tf_op jit(solution)/shard_map/reshape | solution.py:121
  3.4 25.4 %all_to_all.15 = bf16[128,2,384]{2,1,0:T(2,128)(2,1)S(1)} all-to-all(bf16[128,2,384]{2,1,0:T(2,128)(2,1)S(1)} %reshape.26), channel_id=1, replica_groups=mesh['seq'=128,'batch'=4] {'seq'}, dimensions={0} | all-to-all | bytes 393216 | tf_op jit(solution)/shard_map/all_to_all | solution.py:122
  28.7 0.7 copy.14
  29.4 3.5 %shard_map.130 = bf16[128,768]{1,0:T(8,128)(2,1)} custom-call(bf16[128,768]{1,0:T(8,128)(2,1)} %bitcast.16, bf16[256,128]{1,0:T(8,128)(2,1)} %constant.14.clone.refs_1_, bf16[128,256]{1,0:T(8,128)(2,1)} %constant.15.clone.refs_2_, f32[128,512]{1,0:T(8,128)} %constant.16.clone.refs_3_, bf16[512,512]{1,0:T(8,128)(2,1)} %constant.17.clone.refs_4_, ...), custom_call_target="tpu_custom_call" | custom-call | flops 251658240 | bytes 393216 | tf_op jit(solution)/shard_map/pallas_call | solution.py:142
  32.9 1.0 %reshape.28 = bf16[128,2,384]{2,1,0:T(2,128)(2,1)S(1)} reshape(bf16[128,768]{1,0:T(8,128)(2,1)} %shard_map.130) | data formatting | bytes 393216 | tf_op jit(solution)/shard_map/reshape | solution.py:121
  33.9 18.0 %all_to_all.16 = bf16[128,2,384]{2,1,0:T(2,128)(2,1)S(1)} all-to-all(bf16[128,2,384]{2,1,0:T(2,128)(2,1)S(1)} %reshape.28), channel_id=1, replica_groups=mesh['seq'=128,'batch'=4] {'seq'}, dimensions={0} | all-to-all | bytes 393216 | tf_op jit(solution)/shard_map/all_to_all | solution.py:122
  51.9 0.0 copy-start
  51.9 0.6 maximum_reduce_fusion
  52.6 12.1 %all-to-all-start.2 = ((bf16[4,16,256]{2,1,0:T(8,128)(2,1)}), bf16[4,16,256]{2,1,0:T(8,128)(2,1)S(1)}, u32[]{:S(2)}, u32[]{:S(2)}) async-start(bf16[4,16,256]{2,1,0:T(8,128)(2,1)} %bitcast.9), calls=%async_computation.2 | async-start | bytes 65536 | tf_op jit(solution)/shard_map/all_to_all | solution.py:148
  64.7 0.0 copy-done
  64.7 1.8 %shard_map.131 = (bf16[256,128]{1,0:T(8,128)(2,1)}, bf16[256,128]{1,0:T(8,128)(2,1)}, bf16[256,128]{1,0:T(8,128)(2,1)}) custom-call(bf16[256,128]{1,0:T(8,128)(2,1)} %bitcast.20, bf16[256,128]{1,0:T(8,128)(2,1)} %bitcast.22, bf16[256,128]{1,0:T(8,128)(2,1)} %bitcast.24, bf16[128,768]{1,0:T(8,128)(2,1)} %bitcast.15), custom_call_target="tpu_custom_call" | custom-call | flops 393216 | bytes 655360 | tf_op jit(solution)/shard_map/pallas_call | solution.py:155
  66.5 9.7 %all-to-all-done.2 = bf16[4,16,256]{2,1,0:T(8,128)(2,1)S(1)} async-done(((bf16[4,16,256]{2,1,0:T(8,128)(2,1)}), bf16[4,16,256]{2,1,0:T(8,128)(2,1)S(1)}, u32[]{:S(2)}, u32[]{:S(2)}) %all-to-all-start.2) | async-done | bytes 32800 | tf_op jit(solution)/shard_map/all_to_all | solution.py:148
  76.2 0.6 convert_reduce_fusion
  (2 shorter events, 0.0 us)
Async XLA Ops:
  51.9 12.8 %copy-start = (bf16[16,8,2,384]{3,1,2,0:T(8,128)(2,1)}, bf16[16,8,2,384]{3,1,2,0:T(8,128)(2,1)S(1)}, u32[]{:S(2)}) copy-start(bf16[16,8,2,384]{3,1,2,0:T(8,128)(2,1)S(1)} %copy.15) | copy-start | bytes 589828
  52.6 23.6 %all-to-all-start.2 = ((bf16[4,16,256]{2,1,0:T(8,128)(2,1)}), bf16[4,16,256]{2,1,0:T(8,128)(2,1)S(1)}, u32[]{:S(2)}, u32[]{:S(2)}) async-start(bf16[4,16,256]{2,1,0:T(8,128)(2,1)} %bitcast.9), calls=%async_computation.2 | async-start | bytes 65536 | tf_op jit(solution)/shard_map/all_to_all | solution.py:148
where the time goes:
time: 77.2 us; the launch traced here: 76.8 us
  blocking collectives  43.3 us (56%)
  starting transfers between devices  12.1 us (16%)
  waiting for transfers between devices  9.71 us (13%)
  Pallas kernels  7.07 us (9%)
  local copies, waits for them, and re-layouts  2.68 us (3%)
  other arithmetic  1.26 us (2%)
    all_to_all x2, blocking collectives, to_all(): x = lax.all_to_all(x, 'seq', split_axis=0, concat_axis=0, tiled=True)  43.3 us
    all_to_all x1, starting transfers between devices, body(): lax.all_to_all(parts, 'batch', split_axis=0, concat_axis=0, tiled=True)  12.1 us
    all_to_all x1, waiting for transfers between devices, body(): lax.all_to_all(parts, 'batch', split_axis=0, concat_axis=0, tiled=True)  9.71 us
    pallas_call x1, Pallas kernels, body(): back = to_all(transform(sent, first, first_t, turn, inner, inner_t))  3.51 us
    reshape x2, local copies, waits for them, and re-layouts, to_all(): x = x.reshape(x.shape[0], 2, wide // 2)  1.95 us
    pallas_call x1, Pallas kernels, body(): grads = finish(values, gate_in, cotangent, back)  1.81 us
    pallas_call x1, Pallas kernels, body(): sent = to_all(pack(values, gate_in, gate_out, cotangent, filters))  1.75 us
  transfers between devices with their start and end apart: 1, of which 1 were waited for; matrix products, arithmetic and copies ran while one was open for 0% of the time, Pallas kernels for 2%

commit v1 on v0

--- a/solution.py
+++ b/solution.py
@@ -11,12 +11,15 @@
 
 F32 = jnp.float32
 BF16 = jnp.bfloat16
-
-
-def tables(rows, cols):
+VMEM_LIMIT = 12 << 20
+SEQ_FIRST = 2 * 32 + 2 * 8 + 1 * 2
+BATCH_FIRST = 2
+
+
+def tables(rows, cols, order):
     n = rows * cols
     theta = 2.0 * np.pi * np.outer(np.arange(rows) + 0.25, np.arange(rows)) / rows
-    first = np.concatenate([np.cos(theta), -np.sin(theta)], 0)
+    first = np.concatenate([np.cos(theta), -np.sin(theta)], 0)[:, order]
     phi = 2.0 * np.pi * np.outer(np.arange(rows) + 0.25, np.arange(cols)) / n
     turn = np.concatenate([np.cos(phi), np.sin(phi)], 1)
     angle = 2.0 * np.pi * (np.outer(np.arange(cols), np.arange(cols)) % cols) / cols
@@ -39,23 +42,34 @@
     return jnp.dot(a, b, preferred_element_type=F32)
 
 
-def vmem_call(kernel, out_shape, flops, size):
+def vmem_call(kernel, out_shape, flops, size, **kwargs):
     return pl.pallas_call(
         kernel,
         out_shape=out_shape,
+        compiler_params=pltpu.CompilerParams(vmem_limit_bytes=VMEM_LIMIT),
         cost_estimate=pl.CostEstimate(flops=flops, bytes_accessed=size, transcendentals=0),
-    )
-
-
-def gather_kernel(values, gate_in, gate_out, cotangent, filters, out):
+        **kwargs,
+    )
+
+
+def gather_kernel(*refs):
+    sources, out, held, sems = refs[:5], refs[5], refs[6:11], refs[11]
+    copies = [pltpu.make_async_copy(s, h, sems.at[i]) for i, (s, h) in enumerate(zip(sources, held))]
+    for copy in copies:
+        copy.start()
+    filters = held[4]
     half = out.shape[1] // 6
     taps = filters.shape[0]
-    for part, (a, b) in enumerate(((values, gate_in), (cotangent, gate_out))):
+    for part in range(2):
+        a, b = held[2 * part : 2 * part + 2]
+        copies[2 * part].wait()
+        copies[2 * part + 1].wait()
         product = a[...].astype(F32) * b[...].astype(F32)
         for side in range(2):
             piece = product[side * half : (side + 1) * half].T
             at = (3 * side + part) * half
             out[:, at : at + half] = piece.astype(BF16)
+    copies[4].wait()
     for side in range(2):
         piece = filters[:, side * half : (side + 1) * half].astype(BF16)
         at = (3 * side + 2) * half
@@ -107,6 +121,15 @@
         grad_gate_out[at] = (cotangent[at].astype(F32) * conv).astype(BF16)
 
 
+def summed_over_batch(parts):
+    order = [(i + BATCH_FIRST) % len(parts) for i in range(len(parts))]
+    parts = jnp.concatenate([parts[BATCH_FIRST:], parts[:BATCH_FIRST]], axis=0)
+    parts = lax.all_to_all(
+        parts, "batch", split_axis=0, concat_axis=0, tiled=True, axis_index_groups=[order]
+    )
+    return parts.astype(F32).sum(axis=0)
+
+
 def body(values, gate_in, gate_out, cotangent, filters):
     values, gate_in, gate_out, cotangent = (x[0] for x in (values, gate_in, gate_out, cotangent))
     cols, channels = values.shape
@@ -114,12 +137,15 @@
     replicas = lax.axis_size("batch")
     taps = filters.shape[0]
     wide = 3 * cols
-    first, first_t, turn, inner, inner_t = tables(shards, cols)
+    order = [SEQ_FIRST] + [i for i in range(shards) if i != SEQ_FIRST]
+    first, first_t, turn, inner, inner_t = tables(shards, cols, order)
     scale = 1.0 / math.sqrt(channels * replicas // taps * shards * cols)
 
     def to_all(x):
         x = x.reshape(x.shape[0], 2, wide // 2)
-        x = lax.all_to_all(x, "seq", split_axis=0, concat_axis=0, tiled=True)
+        x = lax.all_to_all(
+            x, "seq", split_axis=0, concat_axis=0, tiled=True, axis_index_groups=[order]
+        )
         return x.reshape(x.shape[0], wide)
 
     pack = vmem_call(
@@ -127,8 +153,15 @@
         jax.ShapeDtypeStruct((channels, wide), BF16),
         10 * channels * wide,
         12 * channels * wide,
-    )
-    sent = to_all(pack(values, gate_in, gate_out, cotangent, filters))
+        in_specs=[pl.BlockSpec(memory_space=pltpu.HBM)] * 5,
+        scratch_shapes=[pltpu.VMEM((cols, channels), BF16)] * 4
+        + [pltpu.VMEM((taps, cols), F32), pltpu.SemaphoreType.DMA((5,))],
+    )
+    sources = [
+        pltpu.with_memory_space_constraint(x, pltpu.HBM)
+        for x in (values, gate_in, cotangent, gate_out, filters)
+    ]
+    sent = to_all(pack(*sources))
 
     def spectra(*refs):
         spectra_kernel(scale, *refs)
@@ -145,7 +178,6 @@
     terms = jnp.concatenate([back[:, wide // 2 - half : wide // 2], back[:, wide - half :]], axis=1)
     per_filter = terms.astype(F32).reshape(channels // taps, taps, cols).sum(axis=0)
     parts = per_filter.astype(BF16).reshape(replicas, taps // replicas, cols)
-    parts = lax.all_to_all(parts, "batch", split_axis=0, concat_axis=0, tiled=True)
     finish = vmem_call(
         finish_kernel,
         [jax.ShapeDtypeStruct((cols, channels), BF16)] * 3,
@@ -153,7 +185,7 @@
         20 * cols * channels,
     )
     grads = finish(values, gate_in, cotangent, back)
-    grad_filters = parts.astype(F32).sum(axis=0)
+    grad_filters = summed_over_batch(parts)
     return tuple(x[None] for x in grads) + (grad_filters,)
 
 

time: 77.2 us -> 60.2 us (0.78)
  waiting for transfers between devices: 9.71 us -> 1.3 us
  blocking collectives: 43.3 us -> 38.5 us
  Pallas kernels: 7.07 us -> 3.36 us
  local copies, waits for them, and re-layouts: 2.68 us -> 1.01 us
  starting transfers between devices: 12.1 us -> 13.7 us
    all_to_all x1, waiting for transfers between devices: 9.71 us -> 1.3 us  [summed_over_batch(): lax.all_to_all(parts, 'batch', split_axis=0, concat_axis=0, tiled=True, a...]
    all_to_all x2, blocking collectives: 43.3 us -> 38.5 us  [to_all(): lax.all_to_all(x, 'seq', split_axis=0, concat_axis=0, tiled=True, axis_in...]
    pallas_call x1, Pallas kernels: 3.51 us -> 1.39 us  [body(): back = to_all(transform(sent, first, first_t, turn, inner, inner_t))]
    reshape x2, local copies, waits for them, and re-layouts: 1.95 us -> 0.1 us  [to_all(): x = x.reshape(x.shape[0], 2, wide // 2)]
    all_to_all x1, starting transfers between devices: 12.1 us -> 13.7 us  [summed_over_batch(): lax.all_to_all(parts, 'batch', split_axis=0, concat_axis=0, tiled=True, a...]
    pallas_call x1, Pallas kernels: 1.81 us -> 0.79 us  [body(): grads = finish(values, gate_in, cotangent, back)]
  transfers between devices with their start and end apart: 1 -> 1, of which waited for: 1 -> 1; matrix products, arithmetic and copies ran while one was open for 0% -> 0% of each run, Pallas kernels for 2% -> 1%
where the time goes in v1:
time: 60.2 us; the launch traced here: 59.9 us
  blocking collectives  38.5 us (64%)
  starting transfers between devices  13.7 us (23%)
  Pallas kernels  3.36 us (6%)
  waiting for transfers between devices  1.3 us (2%)
  other arithmetic  1.23 us (2%)
  local copies, waits for them, and re-layouts  1.01 us (2%)
  between operations  0.77 us (1%)
    all_to_all x2, blocking collectives, to_all(): lax.all_to_all(x, 'seq', split_axis=0, concat_axis=0, tiled=True, axis_in...  38.5 us
    all_to_all x1, starting transfers between devices, summed_over_batch(): lax.all_to_all(parts, 'batch', split_axis=0, concat_axis=0, tiled=True, a...  13.7 us
    pallas_call x1, Pallas kernels, body(): back = to_all(transform(sent, first, first_t, turn, inner, inner_t))  1.39 us
    all_to_all x1, waiting for transfers between devices, summed_over_batch(): lax.all_to_all(parts, 'batch', split_axis=0, concat_axis=0, tiled=True, a...  1.3 us
  transfers between devices with their start and end apart: 1, of which 1 were waited for; matrix products, arithmetic and copies ran while one was open for 0% of the time, Pallas kernels for 1%

profile of v1, /device:TPU:1, one launch (start us, length us, event | category | flops | bytes accessed | tf_op | source)
XLA Modules:
  0.0 59.9 jit_solution(18361570175968865706)
XLA Ops:
  0.6 0.0 copy-start.2
  0.6 1.2 %shard_map.129 = bf16[128,768]{1,0:T(8,128)(2,1)S(1)} custom-call(bf16[256,128]{1,0:T(8,128)(2,1)} %bitcast.18, bf16[256,128]{1,0:T(8,128)(2,1)} %bitcast.20, bf16[256,128]{1,0:T(8,128)(2,1)} %bitcast.22, bf16[256,128]{1,0:T(8,128)(2,1)} %bitcast.30, f32[64,256]{1,0:T(8,128)} %refs_4_.2), custom_call_target="tpu_custom_call" | custom-call | flops 983040 | bytes 1179648 | tf_op jit(solution)/shard_map/pallas_call | solution.py:164
  1.8 0.0 copy-start
  1.9 0.0 copy-start.1
  1.9 0.1 reshape.26
  1.9 22.3 %all_to_all.15 = bf16[128,2,384]{2,1,0:T(2,128)(2,1)S(1)} all-to-all(bf16[128,2,384]{2,1,0:T(2,128)(2,1)S(1)} %reshape.26), channel_id=1, replica_groups={{328,0,4,8,12,16,20,24,28,32,36,40,44,48,52,56,60,64,68,72,76,80,84,88,..., dimensions={0} | all-to-all | bytes 393216 | tf_op jit(solution)/shard_map/all_to_all | solution.py:146
  24.2 0.0 copy-start.6
  24.2 0.0 copy-start.7
  24.2 0.0 copy-done.2
  24.2 0.0 copy-done
  24.2 0.0 copy-done.1
  24.2 0.8 %copy-done.6 = bf16[256,128]{1,0:T(8,128)(2,1)S(1)} copy-done((bf16[256,128]{1,0:T(8,128)(2,1)S(1)}, bf16[256,128]{1,0:T(8,128)(2,1)}, u32[]{:S(2)}) %copy-start.6) | copy-done | bytes 65560
  25.0 0.0 copy-done.7
  25.1 1.4 %shard_map.130 = bf16[128,768]{1,0:T(8,128)(2,1)S(1)} custom-call(bf16[128,768]{1,0:T(8,128)(2,1)S(1)} %bitcast.17, bf16[256,128]{1,0:T(8,128)(2,1)S(1)} %copy-done.6, bf16[128,256]{1,0:T(8,128)(2,1)S(1)} %copy-done.7, f32[128,512]{1,0:T(8,128)S(1)} %copy-done.2, bf16[512,512]{1,0:T(8,128)(2,1)S(1)} %copy-done, bf16[512,512]{1,0:T(8,128)(2,1)S(1)} %copy-done.1), custom_call_target="tpu_custom_call" | custom-call | flops 251658240 | bytes 393216 | tf_op jit(solution)/shard_map/pallas_call | solution.py:175
  26.5 0.1 reshape.28
  26.5 16.3 %all_to_all.16 = bf16[128,2,384]{2,1,0:T(2,128)(2,1)S(1)} all-to-all(bf16[128,2,384]{2,1,0:T(2,128)(2,1)S(1)} %reshape.28), channel_id=1, replica_groups={{328,0,4,8,12,16,20,24,28,32,36,40,44,48,52,56,60,64,68,72,76,80,84,88,..., dimensions={0} | all-to-all | bytes 393216 | tf_op jit(solution)/shard_map/all_to_all | solution.py:146
  42.8 0.0 copy-start.5
  42.9 0.0 copy-start.3
  42.9 0.0 copy-start.4
  42.9 0.6 %pad_maximum_fusion = bf16[4,16,256]{2,1,0:T(8,128)(2,1)} fusion(bf16[2,16,256]{2,1,0:T(8,128)(2,1)S(1)} %bitcast.29, bf16[2,16,256]{2,1,0:T(8,128)(2,1)S(1)} %bitcast.28), kind=kLoop, calls=%fused_computation.2 | loop fusion | flops 16384 | bytes 65536 | tf_op jit(solution)/shard_map/concatenate | solution.py:126
  43.5 13.7 %all-to-all-start.2 = ((bf16[4,16,256]{2,1,0:T(8,128)(2,1)}), bf16[4,16,256]{2,1,0:T(8,128)(2,1)S(1)}, u32[]{:S(2)}, u32[]{:S(2)}) async-start(bf16[4,16,256]{2,1,0:T(8,128)(2,1)} %pad_maximum_fusion), calls=%async_computation.2 | async-start | bytes 65536 | tf_op jit(solution)/shard_map/all_to_all | solution.py:127
  57.2 0.0 copy-done.5
  57.2 0.0 copy-done.3
  57.2 0.0 copy-done.4
  57.2 0.8 %shard_map.131 = (bf16[256,128]{1,0:T(8,128)(2,1)}, bf16[256,128]{1,0:T(8,128)(2,1)}, bf16[256,128]{1,0:T(8,128)(2,1)}) custom-call(bf16[256,128]{1,0:T(8,128)(2,1)S(1)} %bitcast.19, bf16[256,128]{1,0:T(8,128)(2,1)S(1)} %bitcast.21, bf16[256,128]{1,0:T(8,128)(2,1)S(1)} %bitcast.23, bf16[128,768]{1,0:T(8,128)(2,1)S(1)} %bitcast.16), custom_call_target="tpu_custom_call" | custom-call | flops 393216 | bytes 655360 | tf_op jit(solution)/shard_map/pallas_call | solution.py:187
  58.0 1.3 %all-to-all-done.2 = bf16[4,16,256]{2,1,0:T(8,128)(2,1)S(1)} async-done(((bf16[4,16,256]{2,1,0:T(8,128)(2,1)}), bf16[4,16,256]{2,1,0:T(8,128)(2,1)S(1)}, u32[]{:S(2)}, u32[]{:S(2)}) %all-to-all-start.2) | async-done | bytes 32800 | tf_op jit(solution)/shard_map/all_to_all | solution.py:127
  59.3 0.6 %convert_reduce_fusion = f32[16,256]{1,0:T(8,128)} fusion(bf16[4,16,256]{2,1,0:T(8,128)(2,1)S(1)} %all-to-all-done.2), kind=kLoop, calls=%fused_computation.1 | loop fusion | flops 28672 | bytes 49152 | tf_op jit(solution)/shard_map/reduce_sum | solution.py:130
  (5 shorter events, 0.1 us)
Async XLA Ops:
  0.6 23.6 %copy-start.2 = (f32[128,512]{1,0:T(8,128)S(1)}, f32[128,512]{1,0:T(8,128)}, u32[]{:S(2)}) copy-start(f32[128,512]{1,0:T(8,128)} %constant.16.clone.refs_3_) | copy-start | bytes 786436
  1.8 22.4 %copy-start = (bf16[512,512]{1,0:T(8,128)(2,1)S(1)}, bf16[512,512]{1,0:T(8,128)(2,1)}, u32[]{:S(2)}) copy-start(bf16[512,512]{1,0:T(8,128)(2,1)} %constant.17.clone.refs_4_) | copy-start | bytes 1572868
  1.9 22.4 %copy-start.1 = (bf16[512,512]{1,0:T(8,128)(2,1)S(1)}, bf16[512,512]{1,0:T(8,128)(2,1)}, u32[]{:S(2)}) copy-start(bf16[512,512]{1,0:T(8,128)(2,1)} %constant.18.clone.refs_5_) | copy-start | bytes 1572868
  24.2 0.8 %copy-start.6 = (bf16[256,128]{1,0:T(8,128)(2,1)S(1)}, bf16[256,128]{1,0:T(8,128)(2,1)}, u32[]{:S(2)}) copy-start(bf16[256,128]{1,0:T(8,128)(2,1)} %constant.14.clone.refs_1_) | copy-start | bytes 196612
  24.2 0.9 %copy-start.7 = (bf16[128,256]{1,0:T(8,128)(2,1)S(1)}, bf16[128,256]{1,0:T(8,128)(2,1)}, u32[]{:S(2)}) copy-start(bf16[128,256]{1,0:T(8,128)(2,1)} %constant.15.clone.refs_2_) | copy-start | bytes 196612
  42.8 14.3 %copy-start.5 = (bf16[1,256,128]{2,1,0:T(8,128)(2,1)S(1)}, bf16[1,256,128]{2,1,0:T(8,128)(2,1)}, u32[]{:S(2)}) copy-start(bf16[1,256,128]{2,1,0:T(8,128)(2,1)} %param.13) | copy-start | bytes 196612
  42.9 14.3 %copy-start.3 = (bf16[1,256,128]{2,1,0:T(8,128)(2,1)S(1)}, bf16[1,256,128]{2,1,0:T(8,128)(2,1)}, u32[]{:S(2)}) copy-start(bf16[1,256,128]{2,1,0:T(8,128)(2,1)} %param.10) | copy-start | bytes 196612
  42.9 14.3 %copy-start.4 = (bf16[1,256,128]{2,1,0:T(8,128)(2,1)S(1)}, bf16[1,256,128]{2,1,0:T(8,128)(2,1)}, u32[]{:S(2)}) copy-start(bf16[1,256,128]{2,1,0:T(8,128)(2,1)} %param.11) | copy-start | bytes 196612
  43.5 15.8 %all-to-all-start.2 = ((bf16[4,16,256]{2,1,0:T(8,128)(2,1)}), bf16[4,16,256]{2,1,0:T(8,128)(2,1)S(1)}, u32[]{:S(2)}, u32[]{:S(2)}) async-start(bf16[4,16,256]{2,1,0:T(8,128)(2,1)} %pad_maximum_fusion), calls=%async_computation.2 | async-start | bytes 65536 | tf_op jit(solution)/shard_map/all_to_all | solution.py:127

commit v2 on v1

--- a/solution.py
+++ b/solution.py
@@ -17,25 +17,16 @@
 
 
 def tables(rows, cols, order):
-    n = rows * cols
     theta = 2.0 * np.pi * np.outer(np.arange(rows) + 0.25, np.arange(rows)) / rows
     first = np.concatenate([np.cos(theta), -np.sin(theta)], 0)[:, order]
-    phi = 2.0 * np.pi * np.outer(np.arange(rows) + 0.25, np.arange(cols)) / n
+    phi = 2.0 * np.pi * np.outer(np.arange(rows) + 0.25, np.arange(cols)) / (rows * cols)
     turn = np.concatenate([np.cos(phi), np.sin(phi)], 1)
     angle = 2.0 * np.pi * (np.outer(np.arange(cols), np.arange(cols)) % cols) / cols
     c, s = np.cos(angle), np.sin(angle)
     inner = np.block([[c, -s], [s, c]])
-
-    def short(a):
-        return a.astype(np.float32).astype(ml_dtypes.bfloat16)
-
-    return (
-        short(first),
-        short(np.ascontiguousarray(first.T)),
-        turn.astype(np.float32),
-        short(inner),
-        short(np.ascontiguousarray(inner.T)),
-    )
+    high = turn.astype(np.float32).astype(ml_dtypes.bfloat16).astype(np.float64)
+    every = [first, first[:rows].T, first[rows:].T, inner, high, turn - high]
+    return np.concatenate(every, 0).astype(np.float32).astype(ml_dtypes.bfloat16)
 
 
 def dot(a, b):
@@ -77,39 +68,42 @@
             out[copy * taps : (copy + 1) * taps, at : at + half] = piece
 
 
-def spectra_kernel(scale, sent, first, first_t, turn, inner, inner_t, out):
-    rows = out.shape[0]
-    cols = out.shape[1] // 3
-    half = cols // 2
+def spectra_kernel(scale, sent, mixing, out):
+    shards = out.shape[0]
+    wide = out.shape[1] // 2
+    cols = wide // 3
+    rows = 2 * shards
+    inner = mixing[4 * rows : 4 * rows + 2 * cols]
+    at = 4 * rows + 2 * cols
+    turn = mixing[at : at + rows].astype(F32) + mixing[at + rows :].astype(F32)
     wc, ws = turn[:, :cols], turn[:, cols:]
-    a = dot(first[...], sent[...])
+    a = dot(mixing[: 2 * rows], jnp.concatenate([sent[:, :wide], sent[:, wide:]], axis=0))
     specs = []
     for j in range(3):
-        at = [slice(j * half, (j + 1) * half), slice((3 + j) * half, (4 + j) * half)]
-        re = jnp.concatenate([a[:rows, at[0]], a[:rows, at[1]]], axis=1)
-        im = jnp.concatenate([a[rows:, at[0]], a[rows:, at[1]]], axis=1)
+        at = slice(j * cols, (j + 1) * cols)
+        re, im = a[:rows, at], a[rows:, at]
         b = jnp.concatenate([re * wc + im * ws, im * wc - re * ws], axis=1)
-        f = dot(b.astype(BF16), inner[...])
+        f = dot(b.astype(BF16), inner)
         specs.append((f[:, :cols], f[:, cols:]))
     (xr, xi), (gr, gi), (hr, hi) = specs
     products = (
-        (hr * xr - hi * xi, hr * xi + hi * xr, 1.0),
-        (hr * gr + hi * gi, hr * gi - hi * gr, 1.0),
-        (xr * gr + xi * gi, xr * gi - xi * gr, scale),
+        (hr * xr - hi * xi, -hr * xi - hi * xr, 1.0),
+        (hr * gr + hi * gi, hi * gr - hr * gi, 1.0),
+        (xr * gr + xi * gi, xi * gr - xr * gi, scale),
     )
-    size = 1.0 / (rows * cols)
     for j, (pr, pi, factor) in enumerate(products):
-        p = jnp.concatenate([pr, pi], axis=1).astype(BF16)
-        u = dot(p, inner_t[...])
+        u = dot(jnp.concatenate([pr, pi], axis=1).astype(BF16), inner)
         ur, ui = u[:, :cols], u[:, cols:]
-        v = jnp.concatenate([ur * wc - ui * ws, ur * ws + ui * wc], axis=0)
-        y = dot(first_t[...], v.astype(BF16)) * (size * factor)
-        for side in range(2):
-            at = (3 * side + j) * half
-            out[:, at : at + half] = y[:, side * half : (side + 1) * half].astype(BF16)
+        vr, vi = ur * wc + ui * ws, ur * ws - ui * wc
+        y = dot(mixing[2 * rows : 3 * rows], vr.astype(BF16))
+        y = y + dot(mixing[3 * rows : 4 * rows], vi.astype(BF16))
+        y = (y * (factor / (rows * cols))).astype(BF16)
+        out[:, j * cols : (j + 1) * cols] = y[:shards]
+        out[:, wide + j * cols : wide + (j + 1) * cols] = y[shards:]
 
 
-def finish_kernel(values, gate_in, cotangent, back, grad_values, grad_gate_in, grad_gate_out):
+def finish_kernel(values, gate_in, cotangent, back, parts, *outs):
+    grad_values, grad_gate_in, grad_gate_out, grad_filters = outs
     half = back.shape[1] // 6
     for side in range(2):
         at = slice(side * half, (side + 1) * half)
@@ -119,15 +113,15 @@
         grad_values[at] = (gate_in[at].astype(F32) * corr).astype(BF16)
         grad_gate_in[at] = (values[at].astype(F32) * corr).astype(BF16)
         grad_gate_out[at] = (cotangent[at].astype(F32) * conv).astype(BF16)
+    grad_filters[...] = parts[...].astype(F32).sum(axis=0)
 
 
-def summed_over_batch(parts):
+def gathered_over_batch(parts):
     order = [(i + BATCH_FIRST) % len(parts) for i in range(len(parts))]
     parts = jnp.concatenate([parts[BATCH_FIRST:], parts[:BATCH_FIRST]], axis=0)
-    parts = lax.all_to_all(
+    return lax.all_to_all(
         parts, "batch", split_axis=0, concat_axis=0, tiled=True, axis_index_groups=[order]
     )
-    return parts.astype(F32).sum(axis=0)
 
 
 def body(values, gate_in, gate_out, cotangent, filters):
@@ -138,7 +132,8 @@
     taps = filters.shape[0]
     wide = 3 * cols
     order = [SEQ_FIRST] + [i for i in range(shards) if i != SEQ_FIRST]
-    first, first_t, turn, inner, inner_t = tables(shards, cols, order)
+    rows = [2 * i + side for side in range(2) for i in order]
+    mixing = tables(2 * shards, cols // 2, rows)
     scale = 1.0 / math.sqrt(channels * replicas // taps * shards * cols)
 
     def to_all(x):
@@ -169,10 +164,10 @@
     transform = vmem_call(
         spectra,
         jax.ShapeDtypeStruct((shards, wide), BF16),
-        4 * shards * wide * (2 * cols + shards),
+        2 * shards * wide * (2 * cols + 4 * shards),
         4 * shards * wide,
     )
-    back = to_all(transform(sent, first, first_t, turn, inner, inner_t))
+    back = to_all(transform(sent, mixing))
 
     half = cols // 2
     terms = jnp.concatenate([back[:, wide // 2 - half : wide // 2], back[:, wide - half :]], axis=1)
@@ -180,12 +175,12 @@
     parts = per_filter.astype(BF16).reshape(replicas, taps // replicas, cols)
     finish = vmem_call(
         finish_kernel,
-        [jax.ShapeDtypeStruct((cols, channels), BF16)] * 3,
+        [jax.ShapeDtypeStruct((cols, channels), BF16)] * 3
+        + [jax.ShapeDtypeStruct((taps // replicas, cols), F32)],
         12 * cols * channels,
         20 * cols * channels,
     )
-    grads = finish(values, gate_in, cotangent, back)
-    grad_filters = summed_over_batch(parts)
+    *grads, grad_filters = finish(values, gate_in, cotangent, back, gathered_over_batch(parts))
     return tuple(x[None] for x in grads) + (grad_filters,)
 
 

time: 60.2 us -> 58.7 us (0.975)
  blocking collectives: 38.5 us -> 54.1 us
  starting transfers between devices: 13.7 us -> 0 us
  waiting for transfers between devices: 1.3 us -> 0 us
  other arithmetic: 1.23 us -> 0.02 us
  local copies, waits for them, and re-layouts: 1.01 us -> 0.19 us
    all_to_all x0 -> x1, blocking collectives: none -> 15.7 us  [gathered_over_batch(): lax.all_to_all(parts, 'batch', split_axis=0, concat_axis=0, tiled=True, a...]
    all_to_all x1 -> x0, starting transfers between devices: 13.7 us -> none  [summed_over_batch(): lax.all_to_all(parts, 'batch', split_axis=0, concat_axis=0, tiled=True, a...]
    all_to_all x1 -> x0, waiting for transfers between devices: 1.3 us -> none  [summed_over_batch(): lax.all_to_all(parts, 'batch', split_axis=0, concat_axis=0, tiled=True, a...]
    unnamed x18 -> x10, local copies, waits for them, and re-layouts: 0.9 us -> 0.07 us
    reduce_sum x1 -> x0, other arithmetic: 0.61 us -> none  [summed_over_batch(): return parts.astype(F32).sum(axis=0)]
  transfers between devices with their start and end apart: 1 -> 0, of which waited for: 1 -> 0; matrix products, arithmetic and copies ran while one was open for 0% -> 0% of each run, Pallas kernels for 1% -> 0%
where the time goes in v2:
time: 58.7 us; the launch traced here: 58.5 us
  blocking collectives  54.1 us (92%)
  Pallas kernels  3.41 us (6%)
  between operations  0.74 us (1%)
    all_to_all x2, blocking collectives, to_all(): lax.all_to_all(x, 'seq', split_axis=0, concat_axis=0, tiled=True, axis_in...  38.4 us
    all_to_all x1, blocking collectives, gathered_over_batch(): lax.all_to_all(parts, 'batch', split_axis=0, concat_axis=0, tiled=True, a...  15.7 us
    pallas_call x1, Pallas kernels, body(): back = to_all(transform(sent, mixing))  1.4 us
    pallas_call x1, Pallas kernels, body(): sent = to_all(pack(*sources))  1.22 us

profile of v2, /device:TPU:1, one launch (start us, length us, event | category | flops | bytes accessed | tf_op | source)
XLA Modules:
  0.0 58.5 jit_solution(16798933991089528024)
XLA Ops:
  0.6 0.0 copy-start
  0.6 1.2 %shard_map.93 = bf16[128,768]{1,0:T(8,128)(2,1)S(1)} custom-call(bf16[256,128]{1,0:T(8,128)(2,1)} %bitcast.18, bf16[256,128]{1,0:T(8,128)(2,1)} %bitcast.20, bf16[256,128]{1,0:T(8,128)(2,1)} %bitcast.22, bf16[256,128]{1,0:T(8,128)(2,1)} %bitcast.30, f32[64,256]{1,0:T(8,128)} %refs_4_.1), custom_call_target="tpu_custom_call" | custom-call | flops 983040 | bytes 1179648 | tf_op jit(solution)/shard_map/pallas_call | solution.py:159
  1.9 0.1 reshape.26
  1.9 22.1 %all_to_all.15 = bf16[128,2,384]{2,1,0:T(2,128)(2,1)S(1)} all-to-all(bf16[128,2,384]{2,1,0:T(2,128)(2,1)S(1)} %reshape.26), channel_id=1, replica_groups={{328,0,4,8,12,16,20,24,28,32,36,40,44,48,52,56,60,64,68,72,76,80,84,88,..., dimensions={0} | all-to-all | bytes 393216 | tf_op jit(solution)/shard_map/all_to_all | solution.py:141
  24.1 0.0 copy-done
  24.1 1.4 %shard_map.94 = bf16[128,768]{1,0:T(8,128)(2,1)S(1)} custom-call(bf16[128,768]{1,0:T(8,128)(2,1)S(1)} %bitcast.17, bf16[1792,256]{1,0:T(8,128)(2,1)S(1)} %copy-done), custom_call_target="tpu_custom_call" | custom-call | flops 201326592 | bytes 393216 | tf_op jit(solution)/shard_map/pallas_call | solution.py:170
  25.5 0.1 reshape.28
  25.6 16.3 %all_to_all.16 = bf16[128,2,384]{2,1,0:T(2,128)(2,1)S(1)} all-to-all(bf16[128,2,384]{2,1,0:T(2,128)(2,1)S(1)} %reshape.28), channel_id=1, replica_groups={{328,0,4,8,12,16,20,24,28,32,36,40,44,48,52,56,60,64,68,72,76,80,84,88,..., dimensions={0} | all-to-all | bytes 393216 | tf_op jit(solution)/shard_map/all_to_all | solution.py:141
  41.9 0.0 copy-start.3
  41.9 0.0 copy-start.1
  41.9 0.0 copy-start.2
  42.0 15.7 %all_to_all.17.parts = bf16[4,16,256]{2,1,0:T(8,128)(2,1)S(1)} all-to-all(bf16[4,16,256]{2,1,0:T(8,128)(2,1)S(1)} %pad_maximum_fusion), channel_id=1, replica_groups={{2,3,0,1},{6,7,4,5},{10,11,8,9},{14,15,12,13},{18,19,16,17},{22,23,20,2..., dimensions={0} | all-to-all | bytes 65536 | tf_op jit(solution)/shard_map/all_to_all | solution.py:122
  57.7 0.0 copy-done.3
  57.7 0.0 copy-done.1
  57.7 0.0 copy-done.2
  57.7 0.8 %shard_map.95 = (bf16[256,128]{1,0:T(8,128)(2,1)}, bf16[256,128]{1,0:T(8,128)(2,1)}, bf16[256,128]{1,0:T(8,128)(2,1)}, f32[16,256]{1,0:T(8,128)}) custom-call(bf16[256,128]{1,0:T(8,128)(2,1)S(1)} %bitcast.19, bf16[256,128]{1,0:T(8,128)(2,1)S(1)} %bitcast.21, bf16[256,128]{1,0:T(8,128)(2,1)S(1)} %bitcast.23, bf16[128,768]{1,0:T(8,128)(2,1)S(1)} %bitcast.16, ...), custom_call_target="tpu_custom_call" | custom-call | flops 393216 | bytes 655360 | tf_op jit(solution)/shard_map/pallas_call | solution.py:183
  (6 shorter events, 0.1 us)
Async XLA Ops:
  0.6 23.5 %copy-start = (bf16[1792,256]{1,0:T(8,128)(2,1)S(1)}, bf16[1792,256]{1,0:T(8,128)(2,1)}, u32[]{:S(2)}) copy-start(bf16[1792,256]{1,0:T(8,128)(2,1)} %constant.5.clone.refs_1_) | copy-start | bytes 2752516
  41.9 15.7 %copy-start.3 = (bf16[1,256,128]{2,1,0:T(8,128)(2,1)S(1)}, bf16[1,256,128]{2,1,0:T(8,128)(2,1)}, u32[]{:S(2)}) copy-start(bf16[1,256,128]{2,1,0:T(8,128)(2,1)} %param.9) | copy-start | bytes 196612
  41.9 15.7 %copy-start.1 = (bf16[1,256,128]{2,1,0:T(8,128)(2,1)S(1)}, bf16[1,256,128]{2,1,0:T(8,128)(2,1)}, u32[]{:S(2)}) copy-start(bf16[1,256,128]{2,1,0:T(8,128)(2,1)} %param.6) | copy-start | bytes 196612
  41.9 15.7 %copy-start.2 = (bf16[1,256,128]{2,1,0:T(8,128)(2,1)S(1)}, bf16[1,256,128]{2,1,0:T(8,128)(2,1)}, u32[]{:S(2)}) copy-start(bf16[1,256,128]{2,1,0:T(8,128)(2,1)} %param.7) | copy-start | bytes 196612
